TPU v7x, 32 devices: a whole 2x2x4 slice. The times are simulated.
32 devices in a mesh: dp: 4 (over z), tp: 8 (over y, x, core).
Axes of the slice: x: 2, y: 2, z: 4, core: 2. Of those that a mesh axis runs over, the one named last changes fastest.
Arguments:
- tokens: bfloat16 [8192, 2048], P(('dp', 'tp')), may hold values from -6 to 6
- segment_ids: int32 [8, 1024], P('dp'), may hold values from 0 to 3, as said below
- prefix_lengths: int32 [8, 4], P('dp'), may hold values from 1 to 512, as said below
- positions: int32 [8, 1024], P('dp'), may hold values from 0 to 511, as said below
- norm_gains: float32 [2, 2048], replicated, may hold values from 0.5 to 1.5
- norm_offsets: float32 [2, 2048], replicated, may hold values from -1.75 to 1.75
- input_weight: bfloat16 [2048, 6144], P(None, 'tp'), may hold values from -0.125 to 0.125
- input_offset: float32 [6144], P('tp'), may hold values from -0.625 to 0.625
- output_weight: bfloat16 [2048, 2048], P('tp'), may hold values from -8 to 8
- output_offset: float32 [2048], replicated, may hold values from -3 to 3
- expand_weight: bfloat16 [2048, 2, 5472], P(None, None, 'tp'), may hold values from -0.125 to 0.125
- expand_offset: float32 [2, 5472], P(None, 'tp'), may hold values from -1.75 to 1.75
- shrink_weight: bfloat16 [5472, 2048], P('tp'), may hold values from -1.25 to 1.25
- shrink_offset: float32 [2048], replicated, may hold values from -3 to 3
- cotangent: bfloat16 [8192, 2048], P(('dp', 'tp')), may hold values from -6 to 6
Outputs:
- layer_out: float32 [8192, 2048], P(('dp', 'tp'))
- tokens_grad: float32 [8192, 2048], P(('dp', 'tp'))
- input_weight_grad: float32 [2048, 6144], P(None, 'tp')
- input_offset_grad: float32 [6144], P('tp')
- output_weight_grad: float32 [2048, 2048], P('tp')
- output_offset_grad: float32 [2048], replicated
- expand_weight_grad: float32 [2048, 2, 5472], P(None, None, 'tp')
- expand_offset_grad: float32 [2, 5472], P(None, 'tp')
- shrink_weight_grad: float32 [5472, 2048], P('tp')
- shrink_offset_grad: float32 [2048], replicated
- norm_gains_grad: float32 [2, 2048], replicated
- norm_offsets_grad: float32 [2, 2048], replicated
Inputs may be any that keep to these rules, and one draw needn't show every extreme that they name: `segment_ids`: each row is one sequence of 4 packed documents: ids never fall, every document has one position or more, one document has exactly 512 positions and the others fewer. `positions`: each token's place within its document, counting from 0. `prefix_lengths`: entry k of a row belongs to document k of that sequence and is at most that document's length; some document has its whole length as prefix, some has a prefix of 1.
All inputs are finite; a program needn't handle non-finite values.
Results may differ from a plain program's by a relative error of at most 0.024.
Values may be sent and summed in bfloat16 or wider, within the bound.
A program may use at most 256 MiB of HBM per device.

v0:
```python
import jax
import jax.numpy as jnp
from jax import lax
from jax.sharding import PartitionSpec as P

HEAD_DIM = 128
FF_USED = 5461
LAYERS = 24
SEQ_LEN = 1024
epsilon = 1e-05
rope_base = 10000.0
masked_score = -1e30


def layer_norm(values, gains, offsets):
    average = jnp.mean(values, axis=-1, keepdims=True)
    centred = values - average
    variance = jnp.mean(centred * centred, axis=-1, keepdims=True)
    return centred * lax.rsqrt(variance + epsilon) * gains + offsets


def rotary_tables(places):
    half_dim = HEAD_DIM // 2
    exponents = lax.iota(jnp.float32, half_dim) * (-2.0 / HEAD_DIM)
    rates = jnp.power(rope_base, exponents)
    angles = places.astype(jnp.float32)[..., None] * rates
    angles = jnp.concatenate([angles, angles], axis=-1)
    return (jnp.cos(angles), jnp.sin(angles))


def rotate(values, cosine, sine):
    half_dim = HEAD_DIM // 2
    turned = jnp.concatenate([-values[..., half_dim:], values[..., :half_dim]], axis=-1)
    return values * cosine + turned * sine


def gated_gelu(gate_up, keep_units):
    return jax.nn.gelu(gate_up[:, 0], approximate=False) * gate_up[:, 1] * keep_units


def visible_mask(segments, places, prefixes):
    doc_count = prefixes.shape[0]
    matches = segments[:, None] == lax.iota(jnp.int32, doc_count)[None, :]
    own_prefix = jnp.sum(jnp.where(matches, prefixes[None, :], 0), axis=1)
    same_doc = segments[:, None] == segments[None, :]
    rows_at = lax.iota(jnp.int32, segments.shape[0])
    earlier = rows_at[None, :] <= rows_at[:, None]
    opened = places[None, :] < own_prefix[:, None]
    return same_doc & (earlier | opened)


def masked_scores(queries, keys_low, segments, places, prefixes):
    visible = visible_mask(segments, places, prefixes)
    scores = jnp.einsum(
        "ihe,jhe->hij", queries, keys_low, preferred_element_type=jnp.float32
    ) * HEAD_DIM ** (-0.5)
    return jnp.where(visible[None], scores, masked_score)


def attend_forward(pieces_in):
    queries, keys_low, values_low, segments, places, prefixes = pieces_in
    scores = masked_scores(queries, keys_low, segments, places, prefixes)
    row_peak = jnp.max(scores, axis=-1, keepdims=True)
    shifted = jnp.exp(scores - row_peak)
    totals = jnp.sum(shifted, axis=-1, keepdims=True)
    attend_probs = (shifted / totals).astype(jnp.bfloat16)
    mixed_heads = jnp.einsum(
        "hij,jhe->ihe", attend_probs, values_low, preferred_element_type=jnp.float32
    )
    return (mixed_heads.astype(jnp.bfloat16), (row_peak + jnp.log(totals))[..., 0])


def attend_backward(pieces_in):
    queries, keys_low, values_low, grad_mixed, log_totals, segments, places, prefixes = pieces_in
    score_scale = HEAD_DIM ** (-0.5)
    scores = masked_scores(queries, keys_low, segments, places, prefixes)
    attend_probs = jnp.exp(scores - log_totals[..., None])
    grad_probs = jnp.einsum(
        "ihe,jhe->hij", grad_mixed, values_low, preferred_element_type=jnp.float32
    )
    grad_values = jnp.einsum(
        "hij,ihe->jhe",
        attend_probs.astype(jnp.bfloat16),
        grad_mixed,
        preferred_element_type=jnp.float32,
    )
    inner_sum = jnp.sum(attend_probs * grad_probs, axis=-1, keepdims=True)
    grad_scores = (attend_probs * (grad_probs - inner_sum)).astype(jnp.bfloat16)
    grad_queries = (
        jnp.einsum("hij,jhe->ihe", grad_scores, keys_low, preferred_element_type=jnp.float32)
        * score_scale
    )
    grad_keys = (
        jnp.einsum("hij,ihe->jhe", grad_scores, queries, preferred_element_type=jnp.float32)
        * score_scale
    )
    return (grad_queries, grad_keys, grad_values)


def local(
    tokens,
    segment_ids,
    prefix_lengths,
    positions,
    norm_gains,
    norm_offsets,
    input_weight,
    input_offset,
    output_weight,
    output_offset,
    expand_weight,
    expand_offset,
    shrink_weight,
    shrink_offset,
    cotangent,
):
    residual_scale = (2.0 * LAYERS) ** 0.5
    seq_count = segment_ids.shape[0]
    group_rows = seq_count * SEQ_LEN
    heads_local = input_weight.shape[1] // (3 * HEAD_DIM)
    width_local = expand_weight.shape[2]
    unit_index = lax.axis_index("tp") * width_local + lax.iota(jnp.int32, width_local)
    keep_units = (unit_index < FF_USED).astype(jnp.float32)
    token_values = tokens.astype(jnp.float32)
    first_norm, first_back = jax.vjp(layer_norm, token_values, norm_gains[0], norm_offsets[0])
    first_low = first_norm.astype(jnp.bfloat16)
    projected = (
        jnp.dot(
            lax.all_gather(first_low, "tp", axis=0, tiled=True),
            input_weight,
            preferred_element_type=jnp.float32,
        )
        + input_offset
    )
    projected = projected.reshape(seq_count, SEQ_LEN, heads_local, 3, HEAD_DIM)
    cosine, sine = rotary_tables(positions)
    cosine = cosine[:, :, None, :]
    sine = sine[:, :, None, :]
    queries = rotate(projected[:, :, :, 0], cosine, sine).astype(jnp.bfloat16)
    keys_low = rotate(projected[:, :, :, 1], cosine, sine).astype(jnp.bfloat16)
    values_low = projected[:, :, :, 2].astype(jnp.bfloat16)
    mixed_heads, log_totals = lax.map(
        attend_forward, (queries, keys_low, values_low, segment_ids, positions, prefix_lengths)
    )
    mixed_low = mixed_heads.reshape(group_rows, heads_local * HEAD_DIM)
    own_heads = lax.all_to_all(mixed_low, "tp", split_axis=0, concat_axis=1, tiled=True)
    full_output = lax.all_gather(output_weight, "tp", axis=0, tiled=True)
    attention_sum = jnp.dot(own_heads, full_output, preferred_element_type=jnp.float32)
    middle = residual_scale * first_norm + attention_sum + output_offset
    second_norm, second_back = jax.vjp(layer_norm, middle, norm_gains[1], norm_offsets[1])
    second_low = second_norm.astype(jnp.bfloat16)
    gate_up = (
        jnp.einsum(
            "id,dcf->icf",
            lax.all_gather(second_low, "tp", axis=0, tiled=True),
            expand_weight,
            preferred_element_type=jnp.float32,
        )
        + expand_offset
    )
    hidden_values, gelu_back = jax.vjp(
        lambda gate_input: gated_gelu(gate_input, keep_units), gate_up
    )
    hidden_low = hidden_values.astype(jnp.bfloat16)
    shrink_sum = lax.psum_scatter(
        jnp.dot(hidden_low, shrink_weight, preferred_element_type=jnp.float32).astype(jnp.bfloat16),
        "tp",
        scatter_dimension=0,
        tiled=True,
    ).astype(jnp.float32)
    layer_out = residual_scale * second_norm + shrink_sum + shrink_offset
    grad_output = cotangent.astype(jnp.float32)
    shrink_offset_grad = jnp.sum(grad_output, axis=0)
    grad_gathered = lax.all_gather(cotangent, "tp", axis=0, tiled=True)
    shrink_weight_grad = jnp.einsum(
        "if,id->fd", hidden_low, grad_gathered, preferred_element_type=jnp.float32
    )
    grad_hidden = jnp.einsum(
        "id,fd->if", grad_gathered, shrink_weight, preferred_element_type=jnp.float32
    )
    grad_gate_up = gelu_back(grad_hidden)[0].astype(jnp.bfloat16)
    expand_offset_grad = jnp.sum(grad_gate_up.astype(jnp.float32), axis=0)
    grad_block = grad_gate_up
    expand_weight_grad = jnp.einsum(
        "id,icf->dcf",
        lax.all_gather(second_low, "tp", axis=0, tiled=True),
        grad_block,
        preferred_element_type=jnp.float32,
    )
    grad_block = grad_gate_up
    grad_second = residual_scale * grad_output + lax.psum_scatter(
        jnp.einsum(
            "icf,dcf->id", grad_block, expand_weight, preferred_element_type=jnp.float32
        ).astype(jnp.bfloat16),
        "tp",
        scatter_dimension=0,
        tiled=True,
    ).astype(jnp.float32)
    grad_middle, second_gain_grad, second_offset_grad = second_back(grad_second)
    grad_attention = grad_middle.astype(jnp.bfloat16)
    output_offset_grad = jnp.sum(grad_attention.astype(jnp.float32), axis=0)
    attention_gathered = lax.all_gather(grad_attention, "tp", axis=0, tiled=True)
    output_weight_grad = jnp.einsum(
        "ia,id->ad", mixed_low, attention_gathered, preferred_element_type=jnp.float32
    )
    grad_mixed = jnp.einsum(
        "id,ad->ia", attention_gathered, output_weight, preferred_element_type=jnp.float32
    ).astype(jnp.bfloat16)
    grad_mixed = grad_mixed.reshape(seq_count, SEQ_LEN, heads_local, HEAD_DIM)
    grad_queries, grad_keys, grad_values = lax.map(
        attend_backward,
        (
            queries,
            keys_low,
            values_low,
            grad_mixed,
            log_totals,
            segment_ids,
            positions,
            prefix_lengths,
        ),
    )
    grad_projected = jnp.stack(
        [rotate(grad_queries, cosine, -sine), rotate(grad_keys, cosine, -sine), grad_values], axis=3
    )
    grad_projected = grad_projected.reshape(group_rows, heads_local * 3 * HEAD_DIM).astype(
        jnp.bfloat16
    )
    input_offset_grad = jnp.sum(grad_projected.astype(jnp.float32), axis=0)
    grad_block = grad_projected
    input_weight_grad = jnp.einsum(
        "id,ic->dc",
        lax.all_gather(first_low, "tp", axis=0, tiled=True),
        grad_block,
        preferred_element_type=jnp.float32,
    )
    grad_block = grad_projected
    grad_first = residual_scale * grad_middle + lax.psum_scatter(
        jnp.einsum(
            "ic,dc->id", grad_block, input_weight, preferred_element_type=jnp.float32
        ).astype(jnp.bfloat16),
        "tp",
        scatter_dimension=0,
        tiled=True,
    ).astype(jnp.float32)
    tokens_grad, first_gain_grad, first_offset_grad = first_back(grad_first)
    summed_weights = (
        lax.psum(input_weight_grad.astype(jnp.bfloat16), "dp").astype(jnp.float32),
        lax.psum(input_offset_grad.astype(jnp.bfloat16), "dp").astype(jnp.float32),
        lax.psum(output_weight_grad.astype(jnp.bfloat16), "dp").astype(jnp.float32),
        lax.psum(expand_weight_grad.astype(jnp.bfloat16), "dp").astype(jnp.float32),
        lax.psum(expand_offset_grad.astype(jnp.bfloat16), "dp").astype(jnp.float32),
        lax.psum(shrink_weight_grad.astype(jnp.bfloat16), "dp").astype(jnp.float32),
    )
    summed_vectors = lax.psum(
        (
            jnp.stack([first_gain_grad, second_gain_grad]),
            jnp.stack([first_offset_grad, second_offset_grad]),
            output_offset_grad,
            shrink_offset_grad,
        ),
        ("dp", "tp"),
    )
    return (
        layer_out,
        tokens_grad,
        summed_weights[0],
        summed_weights[1],
        summed_weights[2],
        summed_vectors[2],
        summed_weights[3],
        summed_weights[4],
        summed_weights[5],
        summed_vectors[3],
        summed_vectors[0],
        summed_vectors[1],
    )


def solution(mesh):
    in_specs = (
        P(("dp", "tp"), None),
        P("dp", None),
        P("dp", None),
        P("dp", None),
        P(),
        P(),
        P(None, "tp"),
        P("tp"),
        P("tp", None),
        P(),
        P(None, None, "tp"),
        P(None, "tp"),
        P("tp", None),
        P(),
        P(("dp", "tp"), None),
    )
    out_specs = (
        P(("dp", "tp"), None),
        P(("dp", "tp"), None),
        P(None, "tp"),
        P("tp"),
        P("tp", None),
        P(),
        P(None, None, "tp"),
        P(None, "tp"),
        P("tp", None),
        P(),
        P(),
        P(),
    )
    return jax.shard_map(local, mesh=mesh, in_specs=in_specs, out_specs=out_specs, check_vma=False)
```

profile of v0, /device:TPU:0, one launch (start us, length us, event | category | flops | bytes accessed | tf_op | source)
XLA Modules:
  0.0 1277.2 jit_solution(5855190570922395362)
XLA Ops:
  16.7 17.1 %fusion.115 = (f32[2,1024,128]{1,0,2:T(2,128)}, f32[2,1024,128]{1,0,2:T(2,128)}, f32[2,1024,128]{1,0,2:T(2,128)}) fusion(f32[2,1024,64]{1,0,2:T(2,128)S(1)} %broadcast_multiply_fusion), kind=kLoop, calls=%fused_computation.195 | loop fusion | flops 524288 | bytes 3670016 | tf_op jit(solution)/shard_map/neg | solution.py:224
  33.8 38.3 %all-gather.6.cloned.1.call-done = bf16[2048,2048]{1,0:T(8,128)(2,1)} async-done(((bf16[256,2048]{1,0:T(8,128)(2,1)}), bf16[2048,2048]{1,0:T(8,128)(2,1)}) %all-gather.6.cloned.1.call-update) | async-done | bytes 8388624 | tf_op jit(solution)/shard_map/all_gather | solution.py:129
  72.1 10.7 broadcast_add_fusion.1
  82.8 6.8 copy.114
  89.6 9.1 reshape.334
  103.3 4.0 slice_bitcast_fusion.1
  110.1 3.9 fusion.99
  114.0 3.8 copy.118
  121.4 29.4 %while.26 = (s32[]{:T(128)}, bf16[2,1024,2,128]{3,2,1,0:T(2,128)(2,1)}, f32[2,2,1024]{2,1,0:T(2,128)S(1)}, bf16[2,1024,2,128]{1,3,2,0:T(8,128)(2,1)}, s32[2,1024...) while((s32[]{:T(128)}, ...), condition=%wide.region_6.7_spmd, body=%wide.region_2.6_spmd.sunk | while | flops 1104421888 | bytes 37852364 | solution.py:142
  128.3 3.7 fusion.168
  142.9 3.7 fusion.168
  153.4 30.8 %all_to_all.19 = bf16[8,256,256]{2,1,0:T(8,128)(2,1)} all-to-all(bf16[8,256,256]{2,1,0:T(8,128)(2,1)} %all_to_all.14), channel_id=1, replica_groups=mesh['dp'=4,'tp'=8] {'tp'}, dimensions={0} | all-to-all | bytes 2097152 | tf_op jit(solution)/shard_map/all_to_all | solution.py:146
  186.4 6.8 fusion.123
  196.1 11.3 fusion.124
  207.4 45.3 %all-gather.10.cloned.1.call-done = bf16[2048,2048]{1,0:T(8,128)(2,1)} async-done(((bf16[256,2048]{1,0:T(8,128)(2,1)}), bf16[2048,2048]{1,0:T(8,128)(2,1)}) %all-gather.10.cloned.1.call-update) | async-done | bytes 8388624 | tf_op jit(solution)/shard_map/all_gather | solution.py:155
  252.7 19.2 %broadcast_add_fusion = f32[2048,2,684]{0,2,1:T(8,128)S(1)} fusion(f32[2,684]{1,0:T(2,128)S(1)} %copy-done.45, bf16[2048,2,684]{0,1,2:T(2,128)(2,1)} %param.29, bf16[2048,2048]{1,0:T(8,128)(2,1)} %all-gather.10.cloned.1.call-done), kind=kOutput, calls=%fused_computation.110 | convolution fusion | flops 11478417408 | bytes 25204064 | tf_op jit(solution)/shard_map/id,dcf->icf/dot_general | solution.py:153
  271.9 15.2 %multiply_bitcast_fusion = (f32[2048,1,684]{0,2,1:T(8,128)}, f32[2048,684]{0,1:T(8,128)}) fusion(f32[2048,684]{0,1:T(8,128)} %fusion.124, f32[684]{0:T(1024)S(1)} %fusion.111, f32[2048,2,684]{0,2,1:T(8,128)S(1)} %broadcast_add_fusion), kind=kLoop, calls=%fused_computation.96 | loop fusion | flops 92454912 | bytes 22416048 | tf_op jit(solution)/shard_map/transpose(jvp())/broadcast_in_dim | solution.py:38
  287.2 7.5 fusion.60
  294.7 21.5 %bitcast_convert_fusion = bf16[2048,2048]{1,0:T(8,128)(2,1)} fusion(bf16[2048,2,684]{0,1,2:T(2,128)(2,1)} %param.29, f32[2048,1,684]{0,2,1:T(8,128)} %get-tuple-element.338, f32[2048,1,684]{0,2,1:T(8,128)} %get-tuple-element.328), kind=kOutput, calls=%fused_computation.71 | convolution fusion | flops 11485413376 | bytes 25198592 | tf_op jit(solution)/shard_map/icf,dcf->id/dot_general | solution.py:192
  316.3 11.7 convolution_convert_fusion
  328.1 59.7 %reduce-scatter.6.cloned.1.call-done = bf16[256,2048]{1,0:T(8,128)(2,1)} async-done(((bf16[2048,2048]{1,0:T(8,128)(2,1)}), bf16[256,2048]{1,0:T(8,128)(2,1)}) %reduce-scatter.6.cloned.1.call-update) | async-done | bytes 1048592 | tf_op jit(solution)/shard_map/reduce_scatter | solution.py:191
  387.8 3.9 multiply_reduce_fusion.1
  391.6 71.2 %reduce-scatter.4.cloned.1.call-done = bf16[256,2048]{1,0:T(8,128)(2,1)} async-done(((bf16[2048,2048]{1,0:T(8,128)(2,1)}), bf16[256,2048]{1,0:T(8,128)(2,1)}) %reduce-scatter.4.cloned.1.call-update) | async-done | bytes 1048592 | tf_op jit(solution)/shard_map/reduce_scatter | solution.py:165
  462.8 5.1 fusion.119
  471.2 3.7 copy.126
  474.8 50.8 %all-gather.14.cloned.1.call-done = bf16[2048,2048]{1,0:T(8,128)(2,1)} async-done(((bf16[256,2048]{1,0:T(8,128)(2,1)}), bf16[2048,2048]{1,0:T(8,128)(2,1)}) %all-gather.14.cloned.1.call-update) | async-done | bytes 8388624 | tf_op jit(solution)/shard_map/all_gather | solution.py:202
  525.6 7.0 convolution_convert_fusion.5
  534.7 166.2 %while.27 = (s32[]{:T(128)}, f32[2,1024,2,128]{1,0,3,2:T(2,128)}, f32[2,1024,2,128]{1,0,3,2:T(2,128)}, bf16[2,1024,2,128]{1,0,3,2:T(2,128)(2,1)}, bf16[2,1024,2,...) while((s32[]{:T(128)}, f32[2,1024,2,128]{1,0,3,2:T(2,128)}, ...), condition=%wide.region_16.17_spmd, body=%wide.region_13.16_spmd.sunk | while | flops 2721588224 | bytes 171013536 | solution.py:210
  546.2 17.8 %dynamic_update_slice.29 = bf16[2,1024,2,128]{1,0,3,2:T(2,128)(2,1)} dynamic-update-slice(bf16[2,1024,2,128]{1,0,3,2:T(2,128)(2,1)} %get-tuple-element.557, bf16[1,1024,2,128]{1,0,3,2:T(2,128)(2,1)} %copy.201, s32[]{:T(128)S(6)} %copy.220, s32[]{:T(128)} %constant.72.clone.1..sunk, s32[]{:T(128)} %constant.72.clone.1..sunk, s32[]{:T(128)} %constant.72.clone.1..sunk) | dynamic-update-slice | bytes 1048580 | tf_op jit(solution)/shard_map/while/body/jit(dynamic_update_index_in_dim)/dynamic_update_slice | solution.py:210
  564.0 7.1 multiply_reduce_fusion.5
  580.3 18.8 %dynamic_update_slice.28 = f32[2,1024,2,128]{1,0,3,2:T(2,128)} dynamic-update-slice(f32[2,1024,2,128]{1,0,3,2:T(2,128)} %get-tuple-element.556, f32[1,1024,2,128]{1,0,3,2:T(1,128)} %copy.200, s32[]{:T(128)S(6)} %copy.220, s32[]{:T(128)} %constant.72.clone.1..sunk, s32[]{:T(128)} %constant.72.clone.1..sunk, s32[]{:T(128)} %constant.72.clone.1..sunk) | dynamic-update-slice | bytes 2097156 | tf_op jit(solution)/shard_map/while/body/jit(dynamic_update_index_in_dim)/dynamic_update_slice | solution.py:210
  599.1 18.8 %dynamic_update_slice.27 = f32[2,1024,2,128]{1,0,3,2:T(2,128)} dynamic-update-slice(f32[2,1024,2,128]{1,0,3,2:T(2,128)} %get-tuple-element.555, f32[1,1024,2,128]{1,0,3,2:T(1,128)} %copy.199, s32[]{:T(128)S(6)} %copy.220, s32[]{:T(128)} %constant.72.clone.1..sunk, s32[]{:T(128)} %constant.72.clone.1..sunk, s32[]{:T(128)} %constant.72.clone.1..sunk) | dynamic-update-slice | bytes 2097156 | tf_op jit(solution)/shard_map/while/body/jit(dynamic_update_index_in_dim)/dynamic_update_slice | solution.py:210
  629.0 17.8 %dynamic_update_slice.29 = bf16[2,1024,2,128]{1,0,3,2:T(2,128)(2,1)} dynamic-update-slice(bf16[2,1024,2,128]{1,0,3,2:T(2,128)(2,1)} %get-tuple-element.557, bf16[1,1024,2,128]{1,0,3,2:T(2,128)(2,1)} %copy.201, s32[]{:T(128)S(6)} %copy.220, s32[]{:T(128)} %constant.72.clone.1..sunk, s32[]{:T(128)} %constant.72.clone.1..sunk, s32[]{:T(128)} %constant.72.clone.1..sunk) | dynamic-update-slice | bytes 1048580 | tf_op jit(solution)/shard_map/while/body/jit(dynamic_update_index_in_dim)/dynamic_update_slice | solution.py:210
  646.8 7.1 multiply_reduce_fusion.5
  663.2 18.8 %dynamic_update_slice.28 = f32[2,1024,2,128]{1,0,3,2:T(2,128)} dynamic-update-slice(f32[2,1024,2,128]{1,0,3,2:T(2,128)} %get-tuple-element.556, f32[1,1024,2,128]{1,0,3,2:T(1,128)} %copy.200, s32[]{:T(128)S(6)} %copy.220, s32[]{:T(128)} %constant.72.clone.1..sunk, s32[]{:T(128)} %constant.72.clone.1..sunk, s32[]{:T(128)} %constant.72.clone.1..sunk) | dynamic-update-slice | bytes 2097156 | tf_op jit(solution)/shard_map/while/body/jit(dynamic_update_index_in_dim)/dynamic_update_slice | solution.py:210
  682.0 18.8 %dynamic_update_slice.27 = f32[2,1024,2,128]{1,0,3,2:T(2,128)} dynamic-update-slice(f32[2,1024,2,128]{1,0,3,2:T(2,128)} %get-tuple-element.555, f32[1,1024,2,128]{1,0,3,2:T(1,128)} %copy.199, s32[]{:T(128)S(6)} %copy.220, s32[]{:T(128)} %constant.72.clone.1..sunk, s32[]{:T(128)} %constant.72.clone.1..sunk, s32[]{:T(128)} %constant.72.clone.1..sunk) | dynamic-update-slice | bytes 2097156 | tf_op jit(solution)/shard_map/while/body/jit(dynamic_update_index_in_dim)/dynamic_update_slice | solution.py:210
  707.5 6.9 fusion.118
  719.3 9.1 convolution_convert_fusion.1
  728.5 10.8 convolution_convert_fusion.3
  739.2 20.8 %fusion.75 = bf16[2048,2,684]{0,2,1:T(8,128)(2,1)} fusion(bf16[2048,2048]{1,0:T(8,128)(2,1)} %all-gather.10.cloned.1.call-done, f32[2048,1,684]{0,2,1:T(8,128)} %get-tuple-element.338, f32[2048,1,684]{0,2,1:T(8,128)} %get-tuple-element.328), kind=kOutput, calls=%fused_computation.115 | convolution fusion | flops 11484020736 | bytes 25198592 | tf_op jit(solution)/shard_map/id,icf->dcf/dot_general | solution.py:184
  763.4 10.7 convolution_convert_fusion.2
  774.1 4.9 fusion.116
  779.2 11.9 all-reduce.3
  792.2 7.6 reduce-scatter.8.cloned.1.call-done
  804.4 45.3 %all-reduce.2 = (f32[2048]{0:T(1024)}, f32[2048]{0:T(1024)}, f32[2,2048]{1,0:T(2,128)}, f32[2,2048]{1,0:T(2,128)}) all-reduce(f32[2048]{0:T(1024)S(1)} %copy-done.36, f32[2048]{0:T(1024)S(1)} %copy-done.33, f32[2,2048]{1,0:T(2,128)S(1)} %pad_maximum_fusion.1, ...), channel_id=1, replica_groups=mesh['dp'=4,'tp'=8] {'dp','tp'}, use_global_device_ids=true, to_apply=%region_25.26 | all-reduce | flops 12288 | bytes 98304 | tf_op jit(solution)/shard_map/psum | solution.py:255
  849.7 3.9 broadcast_add_fusion.2
  853.6 380.8 %all-reduce.7.cloned.1.call-done = (bf16[2048,2,684]{0,2,1:T(8,128)(2,1)}, bf16[2048,768]{1,0:T(8,128)(2,1)}, bf16[256,2048]{1,0:T(8,128)(2,1)}, bf16[684,2048]{1,0:T(8,128)(2,1)}) async-done(((bf16[2048,2,684]{0,2,1:T(8,128)(2,1)}, bf16[2048,768]{1,0:T(8,128)(2,1)}, bf16[256,2048]{1,0:T(8,128)(2,1)}, bf16[684,2048]{1,0:T(8,128)(2,1)}), (bf16[2048,2,684]{0,2,1:T(8,128)(2,1)}, bf16[2048,768]{1,0:T(8,128)(2,1)}, ...) | async-done | bytes 12599312 | tf_op jit(solution)/shard_map/psum | solution.py:251
  1237.2 26.6 %copy.137 = f32[2048,2,684]{0,1,2:T(2,128)} copy(bf16[2048,2,684]{0,2,1:T(8,128)(2,1)} %get-tuple-element.317) | data formatting | bytes 16809984
  (237 shorter events, 125.1 us)
Async XLA Ops:
  7.2 64.9 %copy-start = (bf16[2048,768]{1,0:T(8,128)(2,1)S(1)}, bf16[2048,768]{1,0:T(8,128)(2,1)}, u32[]{:S(2)}) copy-start(bf16[2048,768]{1,0:T(8,128)(2,1)} %param.25) | copy-start | bytes 9437188
  7.2 9.2 copy-start.29
  7.2 64.9 %copy-start.46 = (f32[768]{0:T(1024)S(1)}, f32[768]{0:T(1024)}, u32[]{:S(2)}) copy-start(f32[768]{0:T(1024)} %param.26) | copy-start | bytes 9220
  7.2 64.9 %all-gather.6.cloned.1.call-start = ((), (), s32[]{:S(2)}) async-start(), calls=%async_computation.4 | async-start | bytes 9437184 | tf_op jit(solution)/shard_map/all_gather | solution.py:129
  8.9 177.6 %copy-start.31 = (f32[256]{0:T(256)}, f32[256]{0:T(256)S(1)}, u32[]{:S(2)}) copy-start(f32[256]{0:T(256)S(1)} %broadcast_multiply_fusion.2) | copy-start | bytes 3076
  10.5 5.9 copy-start.41
  10.5 175.9 %copy-start.37 = (f32[256]{0:T(256)}, f32[256]{0:T(256)S(1)}, u32[]{:S(2)}) copy-start(f32[256]{0:T(256)S(1)} %fusion.112) | copy-start | bytes 3076
  11.4 175.1 %copy-start.27 = (f32[1,2048]{1,0:T(1,128)}, f32[1,2048]{1,0:T(1,128)S(1)}, u32[]{:S(2)}) copy-start(f32[1,2048]{1,0:T(1,128)S(1)} %get-tuple-element.359) | copy-start | bytes 24580
  14.9 171.5 %all-gather.8.cloned.1.call-start = ((), (), s32[]{:S(2)}) async-start(), calls=%async_computation.5 | async-start | bytes 9437184 | tf_op jit(solution)/shard_map/all_gather | solution.py:147
  15.6 180.5 %all-gather.12.cloned.1.call-start = ((), (), s32[]{:S(2)}) async-start(), calls=%async_computation.8 | async-start | bytes 9437184 | tf_op jit(solution)/shard_map/all_gather | solution.py:174
  16.4 236.4 %all-gather.10.cloned.1.call-start = ((), (), s32[]{:S(2)}) async-start(), calls=%async_computation.6 | async-start | bytes 9437184 | tf_op jit(solution)/shard_map/all_gather | solution.py:155
  103.3 5.7 slice-start
  110.1 11.3 copy-start.30
  110.1 11.3 copy-start.47
  150.8 35.6 %copy-start.43 = (f32[2048]{0:T(1024)S(1)}, f32[2048]{0:T(1024)}, u32[]{:S(2)}) copy-start(f32[2048]{0:T(1024)} %param.28) | copy-start | bytes 24580
  196.0 191.7 %reduce-scatter.6.cloned.1.call-start = ((), (), s32[]{:S(2)}) async-start(), calls=%async_computation.9 | async-start | bytes 9437184 | tf_op jit(solution)/shard_map/reduce_scatter | solution.py:191
  196.1 56.6 %copy-start.45 = (f32[2,684]{1,0:T(2,128)S(1)}, f32[2,684]{1,0:T(2,128)}, u32[]{:S(2)}) copy-start(f32[2,684]{1,0:T(2,128)} %param.30) | copy-start | bytes 16420
  271.9 15.3 %copy-start.10 = (f32[2048,684]{0,1:T(8,128)S(1)}, f32[2048,684]{0,1:T(8,128)}, u32[]{:S(2)}) copy-start(f32[2048,684]{0,1:T(8,128)} %fusion.124) | copy-start | bytes 16809988
  316.3 146.5 %reduce-scatter.4.cloned.1.call-start = ((), (), s32[]{:S(2)}) async-start(), calls=%async_computation.7 | async-start | bytes 9437184 | tf_op jit(solution)/shard_map/reduce_scatter | solution.py:165
  328.0 134.8 %copy-start.44 = (f32[2048]{0:T(1024)S(1)}, f32[2048]{0:T(1024)}, u32[]{:S(2)}) copy-start(f32[2048]{0:T(1024)} %param.32) | copy-start | bytes 24580
  328.0 197.6 %all-gather.14.cloned.1.call-start = ((), (), s32[]{:S(2)}) async-start(), calls=%async_computation.10 | async-start | bytes 9437184 | tf_op jit(solution)/shard_map/all_gather | solution.py:202
  467.9 64.7 %copy-start.39 = (f32[256]{0:T(256)}, f32[256]{0:T(256)S(1)}, u32[]{:S(2)}) copy-start(f32[256]{0:T(256)S(1)} %negate_multiply_fusion.2) | copy-start | bytes 3076
  471.1 328.8 %reduce-scatter.8.cloned.1.call-start = ((), (), s32[]{:S(2)}) async-start(), calls=%async_computation.11 | async-start | bytes 9437184 | tf_op jit(solution)/shard_map/reduce_scatter | solution.py:238
  536.7 7.2 copy-start.6
  538.1 5.7 copy-start.3
  541.0 3.4 copy-start.1
  564.0 7.1 copy-start.2
  564.0 7.1 copy-start.4
  619.5 7.2 copy-start.6
  621.0 5.7 copy-start.3
  623.8 3.4 copy-start.1
  646.8 7.1 copy-start.2
  646.8 7.1 copy-start.4
  701.0 3.4 copy-start.19
  728.4 506.0 %all-reduce.7.cloned.1.call-start = ((), (), s32[]{:S(2)}) async-start(), calls=%async_computation.12 | async-start | bytes 25296896 | tf_op jit(solution)/shard_map/psum | solution.py:251
  728.5 31.6 %slice-start.2 = ((s8[8388608]{0:T(1024)(128)(4,1)}), s8[4194304]{0:T(1024)(128)(4,1)S(1)}, s32[]{:S(2)}) async-start(s8[8388608]{0:T(1024)(128)(4,1)} %bitcast.266), calls=%async_computation.15 | async-start | bytes 8388608
  739.2 20.8 %slice-start.3 = ((s8[8388608]{0:T(1024)(128)(4,1)}), s8[4194304]{0:T(1024)(128)(4,1)S(1)}, s32[]{:S(2)}) async-start(s8[8388608]{0:T(1024)(128)(4,1)} %bitcast.266), calls=%async_computation.16 | async-start | bytes 8388608
  739.2 20.8 %copy-start.18 = (bf16[2,1024,2,128]{3,2,1,0:T(2,128)(2,1)S(1)}, bf16[2,1024,2,128]{3,2,1,0:T(2,128)(2,1)}, u32[]{:S(2)}) copy-start(bf16[2,1024,2,128]{3,2,1,0:T(2,128)(2,1)} %get-tuple-element.124) | copy-start | bytes 3145732
  774.1 25.7 %copy-start.28 = (f32[1,2048]{1,0:T(1,128)S(1)}, f32[1,2048]{1,0:T(1,128)}, u32[]{:S(2)}) copy-start(f32[1,2048]{1,0:T(1,128)} %copy-done.27) | copy-start | bytes 24580
  774.1 25.7 %copy-start.32 = (f32[256]{0:T(256)S(1)}, f32[256]{0:T(256)}, u32[]{:S(2)}) copy-start(f32[256]{0:T(256)} %copy-done.31) | copy-start | bytes 3076
  774.1 25.7 %copy-start.40 = (f32[256]{0:T(256)S(1)}, f32[256]{0:T(256)}, u32[]{:S(2)}) copy-start(f32[256]{0:T(256)} %copy-done.39) | copy-start | bytes 3076
  779.1 24.0 %copy-start.42 = (f32[256]{0:T(256)S(1)}, f32[256]{0:T(256)}, u32[]{:S(2)}) copy-start(f32[256]{0:T(256)} %copy-done.41) | copy-start | bytes 3076
  779.1 24.0 %copy-start.35 = (f32[2048]{0:T(1024)S(1)}, f32[2048]{0:T(1024)}, u32[]{:S(2)}) copy-start(f32[2048]{0:T(1024)} %get-tuple-element.267) | copy-start | bytes 24580
  779.1 24.0 %copy-start.38 = (f32[256]{0:T(256)S(1)}, f32[256]{0:T(256)}, u32[]{:S(2)}) copy-start(f32[256]{0:T(256)} %copy-done.37) | copy-start | bytes 3076
  779.1 25.3 %copy-start.34 = (f32[2048]{0:T(1024)S(1)}, f32[2048]{0:T(1024)}, u32[]{:S(2)}) copy-start(f32[2048]{0:T(1024)} %get-tuple-element.261) | copy-start | bytes 24580
  779.1 25.3 %copy-start.33 = (f32[2048]{0:T(1024)S(1)}, f32[2048]{0:T(1024)}, u32[]{:S(2)}) copy-start(f32[2048]{0:T(1024)} %get-tuple-element.268) | copy-start | bytes 24580
  779.1 25.3 %copy-start.36 = (f32[2048]{0:T(1024)S(1)}, f32[2048]{0:T(1024)}, u32[]{:S(2)}) copy-start(f32[2048]{0:T(1024)} %get-tuple-element.321) | copy-start | bytes 24580
  1237.2 26.6 %copy-start.24 = (bf16[684,2048]{1,0:T(8,128)(2,1)S(1)}, bf16[684,2048]{1,0:T(8,128)(2,1)}, u32[]{:S(2)}) copy-start(bf16[684,2048]{1,0:T(8,128)(2,1)} %get-tuple-element.320) | copy-start | bytes 8404996
  (21 other events, 47.9 us)
Sparse Core Ops, SparseCore 0:
  15.0 57.0 all-gather.5
  74.0 54.3 all-gather.7
  130.3 65.6 all-gather.11
  198.3 54.3 all-gather.9
  316.4 71.3 reduce-scatter.5
  391.5 71.2 reduce-scatter.3
  471.2 54.3 all-gather.13
  728.5 71.2 reduce-scatter.7
  803.0 431.3 all-reduce.6
where the time goes:
time: 1300 us; the launch traced here: 1280 us
  waiting for transfers between devices  655 us (50%)
  local copies, waits for them, and re-layouts  215 us (17%)
  matrix products  187 us (14%)
  other arithmetic  116 us (9%)
  blocking collectives  87.9 us (7%)
  between operations  14.9 us (1%)
    psum x1, waiting for transfers between devices, local(): lax.psum(expand_weight_grad.astype(jnp.bfloat16), 'dp').astype(jnp.float32)  381 us
    dynamic_update_slice x12, local copies, waits for them, and re-layouts, local(): lax.map(attend_backward, (queries, keys_low, values_low, grad_mixed, log_...  123 us
    reduce_scatter x1, waiting for transfers between devices, local(): lax.psum_scatter(jnp.dot(hidden_low, shrink_weight, preferred_element_typ...  71.2 us
    reduce_scatter x1, waiting for transfers between devices, local(): lax.psum_scatter(jnp.einsum('icf,dcf->id', grad_block, expand_weight, pre...  59.7 us
    all_gather x1, waiting for transfers between devices, local(): lax.all_gather(grad_attention, 'tp', axis=0, tiled=True)  50.8 us
    all_gather x1, waiting for transfers between devices, local(): lax.all_gather(second_low, 'tp', axis=0, tiled=True)  45.3 us
    psum x1, blocking collectives, local(): lax.psum((jnp.stack([first_gain_grad, second_gain_grad]), jnp.stack([firs...  45.3 us
    all_gather x1, waiting for transfers between devices, local(): lax.all_gather(first_low, 'tp', axis=0, tiled=True)  38.3 us
  transfers between devices with their start and end apart: 9, of which 7 were waited for; matrix products, arithmetic and copies ran while one was open for 15% of the time, Pallas kernels for 0%

commit v1 on v0

--- a/solution.py
+++ b/solution.py
@@ -248,7 +248,9 @@
         lax.psum(input_weight_grad.astype(jnp.bfloat16), "dp").astype(jnp.float32),
         lax.psum(input_offset_grad.astype(jnp.bfloat16), "dp").astype(jnp.float32),
         lax.psum(output_weight_grad.astype(jnp.bfloat16), "dp").astype(jnp.float32),
-        lax.psum(expand_weight_grad.astype(jnp.bfloat16), "dp").astype(jnp.float32),
+        jnp.sum(lax.all_gather(expand_weight_grad.astype(jnp.bfloat16), "dp"), axis=0).astype(
+            jnp.float32
+        ),
         lax.psum(expand_offset_grad.astype(jnp.bfloat16), "dp").astype(jnp.float32),
         lax.psum(shrink_weight_grad.astype(jnp.bfloat16), "dp").astype(jnp.float32),
     )

time: 1300 us -> 1310 us (level)
  waiting for transfers between devices: 655 us -> 516 us
  other arithmetic: 116 us -> 237 us
  local copies, waits for them, and re-layouts: 215 us -> 247 us
    psum x1, waiting for transfers between devices: 381 us -> 68 us  [local(): lax.psum(input_weight_grad.astype(jnp.bfloat16), 'dp').astype(jnp.float32)]
    all_gather x0 -> x1, waiting for transfers between devices: none -> 148 us  [local(): lax.all_gather(expand_weight_grad.astype(jnp.bfloat16), 'dp')]
    reduce_sum x0 -> x1, other arithmetic: none -> 120 us  [local(): jnp.sum(lax.all_gather(expand_weight_grad.astype(jnp.bfloat16), 'dp'), ax...]
    reduce_scatter x1, waiting for transfers between devices: 7.62 us -> 62.4 us  [local(): lax.psum_scatter(jnp.einsum('ic,dc->id', grad_block, input_weight, prefer...]
    all_gather x0 -> x1, local copies, waits for them, and re-layouts: none -> 34 us  [local(): lax.all_gather(expand_weight_grad.astype(jnp.bfloat16), 'dp')]
    all_gather x1, waiting for transfers between devices: 50.8 us -> 21.2 us  [local(): lax.all_gather(grad_attention, 'tp', axis=0, tiled=True)]
    unnamed x90 -> x98, local copies, waits for them, and re-layouts: 34.1 us -> 32.5 us
  transfers between devices with their start and end apart: 9 -> 10, of which waited for: 7 -> 8; matrix products, arithmetic and copies ran while one was open for 15% -> 45% of each run, Pallas kernels for 0% -> 0%
where the time goes in v1:
time: 1310 us; the launch traced here: 1290 us
  waiting for transfers between devices  516 us (39%)
  local copies, waits for them, and re-layouts  247 us (19%)
  other arithmetic  237 us (18%)
  matrix products  184 us (14%)
  blocking collectives  85.9 us (7%)
  between operations  15.3 us (1%)
    all_gather x1, waiting for transfers between devices, local(): lax.all_gather(expand_weight_grad.astype(jnp.bfloat16), 'dp')  148 us
    dynamic_update_slice x12, local copies, waits for them, and re-layouts, local(): lax.map(attend_backward, (queries, keys_low, values_low, grad_mixed, log_...  123 us
    reduce_sum x1, other arithmetic, local(): jnp.sum(lax.all_gather(expand_weight_grad.astype(jnp.bfloat16), 'dp'), ax...  120 us
    reduce_scatter x1, waiting for transfers between devices, local(): lax.psum_scatter(jnp.dot(hidden_low, shrink_weight, preferred_element_typ...  71.2 us
    psum x1, waiting for transfers between devices, local(): lax.psum(input_weight_grad.astype(jnp.bfloat16), 'dp').astype(jnp.float32)  68 us
    reduce_scatter x1, waiting for transfers between devices, local(): lax.psum_scatter(jnp.einsum('ic,dc->id', grad_block, input_weight, prefer...  62.4 us
    reduce_scatter x1, waiting for transfers between devices, local(): lax.psum_scatter(jnp.einsum('icf,dcf->id', grad_block, expand_weight, pre...  59.8 us
    all_gather x1, waiting for transfers between devices, local(): lax.all_gather(second_low, 'tp', axis=0, tiled=True)  45.5 us
  transfers between devices with their start and end apart: 10, of which 8 were waited for; matrix products, arithmetic and copies ran while one was open for 45% of the time, Pallas kernels for 0%

profile of v1, /device:TPU:0, one launch (start us, length us, event | category | flops | bytes accessed | tf_op | source)
XLA Modules:
  0.0 1286.9 jit_solution(2034319828500615753)
XLA Ops:
  16.7 17.1 %fusion.115 = (f32[2,1024,128]{1,0,2:T(2,128)}, f32[2,1024,128]{1,0,2:T(2,128)}, f32[2,1024,128]{1,0,2:T(2,128)}) fusion(f32[2,1024,64]{1,0,2:T(2,128)S(1)} %broadcast_multiply_fusion), kind=kLoop, calls=%fused_computation.195 | loop fusion | flops 524288 | bytes 3670016 | tf_op jit(solution)/shard_map/neg | solution.py:224
  33.8 38.3 %all-gather.8.cloned.1.call-done = bf16[2048,2048]{1,0:T(8,128)(2,1)} async-done(((bf16[256,2048]{1,0:T(8,128)(2,1)}), bf16[2048,2048]{1,0:T(8,128)(2,1)}) %all-gather.8.cloned.1.call-update) | async-done | bytes 8388624 | tf_op jit(solution)/shard_map/all_gather | solution.py:129
  72.1 10.7 broadcast_add_fusion.1
  82.8 6.8 copy.112
  89.6 9.1 reshape.334
  103.3 4.0 slice_bitcast_fusion.1
  110.1 3.9 fusion.99
  114.0 3.8 copy.116
  121.5 29.3 %while.26 = (s32[]{:T(128)}, bf16[2,1024,2,128]{3,2,1,0:T(2,128)(2,1)}, f32[2,2,1024]{2,1,0:T(2,128)S(1)}, bf16[2,1024,2,128]{1,3,2,0:T(8,128)(2,1)}, s32[2,1024...) while((s32[]{:T(128)}, ...), condition=%wide.region_6.7_spmd, body=%wide.region_2.6_spmd.sunk | while | flops 1104421888 | bytes 37852364 | solution.py:142
  153.3 30.8 %all_to_all.19 = bf16[8,256,256]{2,1,0:T(8,128)(2,1)} all-to-all(bf16[8,256,256]{2,1,0:T(8,128)(2,1)} %all_to_all.14), channel_id=1, replica_groups=mesh['dp'=4,'tp'=8] {'tp'}, dimensions={0} | all-to-all | bytes 2097152 | tf_op jit(solution)/shard_map/all_to_all | solution.py:146
  186.4 6.8 fusion.123
  196.1 11.1 fusion.124
  207.2 45.5 %all-gather.12.cloned.1.call-done = bf16[2048,2048]{1,0:T(8,128)(2,1)} async-done(((bf16[256,2048]{1,0:T(8,128)(2,1)}), bf16[2048,2048]{1,0:T(8,128)(2,1)}) %all-gather.12.cloned.1.call-update) | async-done | bytes 8388624 | tf_op jit(solution)/shard_map/all_gather | solution.py:155
  252.7 19.2 %broadcast_add_fusion = f32[2048,2,684]{0,2,1:T(8,128)S(1)} fusion(f32[2,684]{1,0:T(2,128)S(1)} %copy-done.46, bf16[2048,2,684]{0,1,2:T(2,128)(2,1)} %param.29, bf16[2048,2048]{1,0:T(8,128)(2,1)} %all-gather.12.cloned.1.call-done), kind=kOutput, calls=%fused_computation.110 | convolution fusion | flops 11478417408 | bytes 25204064 | tf_op jit(solution)/shard_map/id,dcf->icf/dot_general | solution.py:153
  271.9 15.2 %multiply_bitcast_fusion = (f32[2048,1,684]{0,2,1:T(8,128)}, f32[2048,684]{0,1:T(8,128)}) fusion(f32[2048,684]{0,1:T(8,128)} %fusion.124, f32[684]{0:T(1024)S(1)} %fusion.111, f32[2048,2,684]{0,2,1:T(8,128)S(1)} %broadcast_add_fusion), kind=kLoop, calls=%fused_computation.96 | loop fusion | flops 92454912 | bytes 22416048 | tf_op jit(solution)/shard_map/transpose(jvp())/broadcast_in_dim | solution.py:38
  287.2 7.8 fusion.60
  295.0 21.5 %bitcast_convert_fusion = bf16[2048,2048]{1,0:T(8,128)(2,1)} fusion(bf16[2048,2,684]{0,1,2:T(2,128)(2,1)} %param.29, f32[2048,1,684]{0,2,1:T(8,128)} %get-tuple-element.313, f32[2048,1,684]{0,2,1:T(8,128)} %get-tuple-element.303), kind=kOutput, calls=%fused_computation.71 | convolution fusion | flops 11485413376 | bytes 25198592 | tf_op jit(solution)/shard_map/icf,dcf->id/dot_general | solution.py:192
  316.6 11.5 convolution_convert_fusion
  328.2 59.8 %reduce-scatter.6.cloned.1.call-done = bf16[256,2048]{1,0:T(8,128)(2,1)} async-done(((bf16[2048,2048]{1,0:T(8,128)(2,1)}), bf16[256,2048]{1,0:T(8,128)(2,1)}) %reduce-scatter.6.cloned.1.call-update) | async-done | bytes 1048592 | tf_op jit(solution)/shard_map/reduce_scatter | solution.py:191
  388.0 3.9 multiply_reduce_fusion.1
  391.9 71.2 %reduce-scatter.4.cloned.1.call-done = bf16[256,2048]{1,0:T(8,128)(2,1)} async-done(((bf16[2048,2048]{1,0:T(8,128)(2,1)}), bf16[256,2048]{1,0:T(8,128)(2,1)}) %reduce-scatter.4.cloned.1.call-update) | async-done | bytes 1048592 | tf_op jit(solution)/shard_map/reduce_scatter | solution.py:165
  463.0 5.1 fusion.119
  471.3 19.1 %fusion.75 = bf16[2048,2,684]{0,2,1:T(8,128)(2,1)} fusion(bf16[2048,2048]{1,0:T(8,128)(2,1)} %all-gather.12.cloned.1.call-done, f32[2048,1,684]{0,2,1:T(8,128)} %get-tuple-element.313, f32[2048,1,684]{0,2,1:T(8,128)} %get-tuple-element.303), kind=kOutput, calls=%fused_computation.115 | convolution fusion | flops 11484020736 | bytes 25198592 | tf_op jit(solution)/shard_map/id,icf->dcf/dot_general | solution.py:184
  494.2 10.4 convolution_convert_fusion.3
  504.6 21.2 %all-gather.16.cloned.1.call-done = bf16[2048,2048]{1,0:T(8,128)(2,1)} async-done(((bf16[256,2048]{1,0:T(8,128)(2,1)}), bf16[2048,2048]{1,0:T(8,128)(2,1)}) %all-gather.16.cloned.1.call-update) | async-done | bytes 8388624 | tf_op jit(solution)/shard_map/all_gather | solution.py:202
  525.8 7.0 convolution_convert_fusion.5
  535.1 166.7 %while.27 = (s32[]{:T(128)}, f32[2,1024,2,128]{1,0,3,2:T(2,128)}, f32[2,1024,2,128]{1,0,3,2:T(2,128)}, bf16[2,1024,2,128]{1,0,3,2:T(2,128)(2,1)}, bf16[2,1024,2,...) while((s32[]{:T(128)}, f32[2,1024,2,128]{1,0,3,2:T(2,128)}, ...), condition=%wide.region_16.17_spmd, body=%wide.region_13.16_spmd.sunk | while | flops 2721588224 | bytes 171013536 | solution.py:210
  546.7 17.8 %dynamic_update_slice.29 = bf16[2,1024,2,128]{1,0,3,2:T(2,128)(2,1)} dynamic-update-slice(bf16[2,1024,2,128]{1,0,3,2:T(2,128)(2,1)} %get-tuple-element.532, bf16[1,1024,2,128]{1,0,3,2:T(2,128)(2,1)} %copy.200, s32[]{:T(128)S(6)} %copy.219, s32[]{:T(128)} %constant.72.clone.1..sunk, s32[]{:T(128)} %constant.72.clone.1..sunk, s32[]{:T(128)} %constant.72.clone.1..sunk) | dynamic-update-slice | bytes 1048580 | tf_op jit(solution)/shard_map/while/body/jit(dynamic_update_index_in_dim)/dynamic_update_slice | solution.py:210
  564.5 7.2 multiply_reduce_fusion.5
  581.0 18.8 %dynamic_update_slice.28 = f32[2,1024,2,128]{1,0,3,2:T(2,128)} dynamic-update-slice(f32[2,1024,2,128]{1,0,3,2:T(2,128)} %get-tuple-element.531, f32[1,1024,2,128]{1,0,3,2:T(1,128)} %copy.199, s32[]{:T(128)S(6)} %copy.219, s32[]{:T(128)} %constant.72.clone.1..sunk, s32[]{:T(128)} %constant.72.clone.1..sunk, s32[]{:T(128)} %constant.72.clone.1..sunk) | dynamic-update-slice | bytes 2097156 | tf_op jit(solution)/shard_map/while/body/jit(dynamic_update_index_in_dim)/dynamic_update_slice | solution.py:210
  599.8 18.8 %dynamic_update_slice.27 = f32[2,1024,2,128]{1,0,3,2:T(2,128)} dynamic-update-slice(f32[2,1024,2,128]{1,0,3,2:T(2,128)} %get-tuple-element.530, f32[1,1024,2,128]{1,0,3,2:T(1,128)} %copy.198, s32[]{:T(128)S(6)} %copy.219, s32[]{:T(128)} %constant.72.clone.1..sunk, s32[]{:T(128)} %constant.72.clone.1..sunk, s32[]{:T(128)} %constant.72.clone.1..sunk) | dynamic-update-slice | bytes 2097156 | tf_op jit(solution)/shard_map/while/body/jit(dynamic_update_index_in_dim)/dynamic_update_slice | solution.py:210
  629.7 17.8 %dynamic_update_slice.29 = bf16[2,1024,2,128]{1,0,3,2:T(2,128)(2,1)} dynamic-update-slice(bf16[2,1024,2,128]{1,0,3,2:T(2,128)(2,1)} %get-tuple-element.532, bf16[1,1024,2,128]{1,0,3,2:T(2,128)(2,1)} %copy.200, s32[]{:T(128)S(6)} %copy.219, s32[]{:T(128)} %constant.72.clone.1..sunk, s32[]{:T(128)} %constant.72.clone.1..sunk, s32[]{:T(128)} %constant.72.clone.1..sunk) | dynamic-update-slice | bytes 1048580 | tf_op jit(solution)/shard_map/while/body/jit(dynamic_update_index_in_dim)/dynamic_update_slice | solution.py:210
  647.5 7.1 multiply_reduce_fusion.5
  663.8 18.8 %dynamic_update_slice.28 = f32[2,1024,2,128]{1,0,3,2:T(2,128)} dynamic-update-slice(f32[2,1024,2,128]{1,0,3,2:T(2,128)} %get-tuple-element.531, f32[1,1024,2,128]{1,0,3,2:T(1,128)} %copy.199, s32[]{:T(128)S(6)} %copy.219, s32[]{:T(128)} %constant.72.clone.1..sunk, s32[]{:T(128)} %constant.72.clone.1..sunk, s32[]{:T(128)} %constant.72.clone.1..sunk) | dynamic-update-slice | bytes 2097156 | tf_op jit(solution)/shard_map/while/body/jit(dynamic_update_index_in_dim)/dynamic_update_slice | solution.py:210
  682.7 18.8 %dynamic_update_slice.27 = f32[2,1024,2,128]{1,0,3,2:T(2,128)} dynamic-update-slice(f32[2,1024,2,128]{1,0,3,2:T(2,128)} %get-tuple-element.530, f32[1,1024,2,128]{1,0,3,2:T(1,128)} %copy.198, s32[]{:T(128)S(6)} %copy.219, s32[]{:T(128)} %constant.72.clone.1..sunk, s32[]{:T(128)} %constant.72.clone.1..sunk, s32[]{:T(128)} %constant.72.clone.1..sunk) | dynamic-update-slice | bytes 2097156 | tf_op jit(solution)/shard_map/while/body/jit(dynamic_update_index_in_dim)/dynamic_update_slice | solution.py:210
  708.5 6.9 fusion.118
  722.4 8.3 convolution_convert_fusion.2
  730.8 10.9 convolution_convert_fusion.1
  741.7 4.9 fusion.116
  746.7 14.6 %all-reduce.3 = (bf16[768]{0:T(1024)(128)(2,1)S(1)}, bf16[2,684]{1,0:T(2,128)(2,1)S(1)}) all-reduce(bf16[768]{0:T(1024)(128)(2,1)S(1)} %reduce_sum.241, bf16[2,684]{1,0:T(2,128)(2,1)S(1)} %fusion.116), channel_id=1, replica_groups=mesh['dp'=4,'tp'=8] {'dp'}, use_global_device_ids=true, to_apply=%region_22.23 | all-reduce | flops 2136 | bytes 8544 | tf_op jit(solution)/shard_map/psum | solution.py:249
  762.5 148.0 %all-gather.18.cloned.1.call-done = bf16[8192,2,684]{0,2,1:T(8,128)(2,1)} async-done(((bf16[2048,2,684]{0,2,1:T(8,128)(2,1)}), bf16[8192,2,684]{0,2,1:T(8,128)(2,1)}) %all-gather.18.cloned.1.call-update) | async-done | bytes 22413328 | tf_op jit(solution)/shard_map/all_gather | solution.py:251
  910.5 34.0 %reshape.341 = bf16[4,2048,2,684]{1,0,3,2:T(4,128)(2,1)} reshape(bf16[8192,2,684]{0,2,1:T(8,128)(2,1)} %all-gather.18.cloned.1.call-done) | data formatting | bytes 44826624 | tf_op jit(solution)/shard_map/all_gather | solution.py:251
  944.5 120.0 %reduce_sum.243 = bf16[2048,2,684]{0,2,1:T(8,128)(2,1)} reduce(bf16[4,2048,2,684]{1,0,3,2:T(4,128)(2,1)} %reshape.341, bf16[]{:T(256)} %constant.73.clone.1), dimensions={0}, to_apply=%region_26.27 | reduce | flops 8404992 | bytes 28016642 | tf_op jit(solution)/shard_map/reduce_sum | solution.py:251
  1064.5 26.4 %copy.135 = f32[2048,2,684]{0,1,2:T(2,128)} copy(bf16[2048,2,684]{0,2,1:T(8,128)(2,1)} %reduce_sum.243) | data formatting | bytes 16809984
  1090.9 68.0 %all-reduce.7.cloned.1.call-done = (bf16[2048,768]{1,0:T(8,128)(2,1)}, bf16[256,2048]{1,0:T(8,128)(2,1)}, bf16[684,2048]{1,0:T(8,128)(2,1)}) async-done(((bf16[2048,768]{1,0:T(8,128)(2,1)}, bf16[256,2048]{1,0:T(8,128)(2,1)}, bf16[684,2048]{1,0:T(8,128)(2,1)}), (bf16[2048,768]{1,0:T(8,128)(2,1)}, bf16[256,2048]{1,0:T(8,128)(2,1)}, bf16[684,2048]{1,0:T(8,128)(2,1)})) %all-reduce.7.cloned.1.call-update) | async-done | bytes 6995984 | tf_op jit(solution)/shard_map/psum | solution.py:248
  1161.9 5.1 convert_element_type.145
  1170.5 62.4 %reduce-scatter.8.cloned.1.call-done = bf16[256,2048]{1,0:T(8,128)(2,1)} async-done(((bf16[2048,2048]{1,0:T(8,128)(2,1)}), bf16[256,2048]{1,0:T(8,128)(2,1)}) %reduce-scatter.8.cloned.1.call-update) | async-done | bytes 1048592 | tf_op jit(solution)/shard_map/reduce_scatter | solution.py:238
  1239.2 40.5 %all-reduce.2 = (f32[2048]{0:T(1024)}, f32[2048]{0:T(1024)}, f32[2,2048]{1,0:T(2,128)}, f32[2,2048]{1,0:T(2,128)}) all-reduce(f32[2048]{0:T(1024)S(1)} %copy-done.37, f32[2048]{0:T(1024)S(1)} %copy-done.34, f32[2,2048]{1,0:T(2,128)S(1)} %pad_maximum_fusion.1, ...), channel_id=1, replica_groups=mesh['dp'=4,'tp'=8] {'dp','tp'}, use_global_device_ids=true, to_apply=%region_25.26 | all-reduce | flops 12288 | bytes 98304 | tf_op jit(solution)/shard_map/psum | solution.py:257
  (251 shorter events, 134.5 us)
Async XLA Ops:
  7.2 64.9 %copy-start = (bf16[2048,768]{1,0:T(8,128)(2,1)S(1)}, bf16[2048,768]{1,0:T(8,128)(2,1)}, u32[]{:S(2)}) copy-start(bf16[2048,768]{1,0:T(8,128)(2,1)} %param.25) | copy-start | bytes 9437188
  7.2 9.2 copy-start.26
  7.2 64.9 %copy-start.47 = (f32[768]{0:T(1024)S(1)}, f32[768]{0:T(1024)}, u32[]{:S(2)}) copy-start(f32[768]{0:T(1024)} %param.26) | copy-start | bytes 9220
  7.2 64.9 %all-gather.8.cloned.1.call-start = ((), (), s32[]{:S(2)}) async-start(), calls=%async_computation.4 | async-start | bytes 9437184 | tf_op jit(solution)/shard_map/all_gather | solution.py:129
  8.9 177.5 %copy-start.32 = (f32[256]{0:T(256)}, f32[256]{0:T(256)S(1)}, u32[]{:S(2)}) copy-start(f32[256]{0:T(256)S(1)} %broadcast_multiply_fusion.2) | copy-start | bytes 3076
  10.5 5.9 copy-start.42
  10.5 175.8 %copy-start.38 = (f32[256]{0:T(256)}, f32[256]{0:T(256)S(1)}, u32[]{:S(2)}) copy-start(f32[256]{0:T(256)S(1)} %fusion.112) | copy-start | bytes 3076
  11.4 175.0 %copy-start.24 = (f32[1,2048]{1,0:T(1,128)}, f32[1,2048]{1,0:T(1,128)S(1)}, u32[]{:S(2)}) copy-start(f32[1,2048]{1,0:T(1,128)S(1)} %get-tuple-element.334) | copy-start | bytes 24580
  14.9 171.5 %all-gather.10.cloned.1.call-start = ((), (), s32[]{:S(2)}) async-start(), calls=%async_computation.5 | async-start | bytes 9437184 | tf_op jit(solution)/shard_map/all_gather | solution.py:147
  15.6 180.5 %all-gather.14.cloned.1.call-start = ((), (), s32[]{:S(2)}) async-start(), calls=%async_computation.8 | async-start | bytes 9437184 | tf_op jit(solution)/shard_map/all_gather | solution.py:174
  16.4 236.4 %all-gather.12.cloned.1.call-start = ((), (), s32[]{:S(2)}) async-start(), calls=%async_computation.6 | async-start | bytes 9437184 | tf_op jit(solution)/shard_map/all_gather | solution.py:155
  103.3 5.7 slice-start
  110.1 11.3 copy-start.28
  110.1 11.3 copy-start.48
  150.8 42.4 %copy-start.30 = (f32[2,2,1024]{2,1,0:T(2,128)}, f32[2,2,1024]{2,1,0:T(2,128)S(1)}, u32[]{:S(2)}) copy-start(f32[2,2,1024]{2,1,0:T(2,128)S(1)} %get-tuple-element.524) | copy-start | bytes 49156
  150.8 35.6 %copy-start.44 = (f32[2048]{0:T(1024)S(1)}, f32[2048]{0:T(1024)}, u32[]{:S(2)}) copy-start(f32[2048]{0:T(1024)} %param.28) | copy-start | bytes 24580
  196.0 192.0 %reduce-scatter.6.cloned.1.call-start = ((), (), s32[]{:S(2)}) async-start(), calls=%async_computation.9 | async-start | bytes 9437184 | tf_op jit(solution)/shard_map/reduce_scatter | solution.py:191
  196.1 56.7 %copy-start.46 = (f32[2,684]{1,0:T(2,128)S(1)}, f32[2,684]{1,0:T(2,128)}, u32[]{:S(2)}) copy-start(f32[2,684]{1,0:T(2,128)} %param.30) | copy-start | bytes 16420
  271.9 15.3 %copy-start.10 = (f32[2048,684]{0,1:T(8,128)S(1)}, f32[2048,684]{0,1:T(8,128)}, u32[]{:S(2)}) copy-start(f32[2048,684]{0,1:T(8,128)} %fusion.124) | copy-start | bytes 16809988
  316.6 146.5 %reduce-scatter.4.cloned.1.call-start = ((), (), s32[]{:S(2)}) async-start(), calls=%async_computation.7 | async-start | bytes 9437184 | tf_op jit(solution)/shard_map/reduce_scatter | solution.py:165
  328.1 134.9 %copy-start.45 = (f32[2048]{0:T(1024)S(1)}, f32[2048]{0:T(1024)}, u32[]{:S(2)}) copy-start(f32[2048]{0:T(1024)} %param.32) | copy-start | bytes 24580
  328.1 197.7 %all-gather.16.cloned.1.call-start = ((), (), s32[]{:S(2)}) async-start(), calls=%async_computation.10 | async-start | bytes 9437184 | tf_op jit(solution)/shard_map/all_gather | solution.py:202
  471.3 439.2 %all-gather.18.cloned.1.call-start = ((), (), s32[]{:S(2)}) async-start(), calls=%async_computation.12 | async-start | bytes 28180480 | tf_op jit(solution)/shard_map/all_gather | solution.py:251
  490.4 668.5 %all-reduce.7.cloned.1.call-start = ((), (), s32[]{:S(2)}) async-start(), calls=%async_computation.13 | async-start | bytes 14024704 | tf_op jit(solution)/shard_map/psum | solution.py:248
  504.6 30.6 %copy-start.27 = (s32[2,1024]{1,0:T(2,128)S(1)}, s32[2,1024]{1,0:T(2,128)}, u32[]{:S(2)}) copy-start(s32[2,1024]{1,0:T(2,128)} %param.22) | copy-start | bytes 24580
  504.6 30.6 %copy-start.29 = (s32[2,1024]{1,0:T(2,128)S(1)}, s32[2,1024]{1,0:T(2,128)}, u32[]{:S(2)}) copy-start(s32[2,1024]{1,0:T(2,128)} %param.20) | copy-start | bytes 24580
  504.6 30.6 %copy-start.31 = (f32[2,2,1024]{2,1,0:T(2,128)S(1)}, f32[2,2,1024]{2,1,0:T(2,128)}, u32[]{:S(2)}) copy-start(f32[2,2,1024]{2,1,0:T(2,128)} %copy-done.30) | copy-start | bytes 49156
  504.6 30.6 %copy-start.49 = (s32[2,4]{1,0:T(2,128)S(1)}, s32[2,4]{1,0:T(2,128)}, u32[]{:S(2)}) copy-start(s32[2,4]{1,0:T(2,128)} %param.21) | copy-start | bytes 100
  537.0 7.3 copy-start.6
  538.5 5.9 copy-start.3
  541.5 3.4 copy-start.1
  564.5 7.2 copy-start.2
  564.5 7.2 copy-start.4
  620.2 7.2 copy-start.6
  621.7 5.7 copy-start.3
  647.5 7.1 copy-start.2
  647.5 7.1 copy-start.4
  701.9 3.5 copy-start.18
  708.4 10.2 slice-start.2
  717.6 4.5 slice-start.4
  718.7 3.7 slice-start.5
  730.7 502.1 %reduce-scatter.8.cloned.1.call-start = ((), (), s32[]{:S(2)}) async-start(), calls=%async_computation.11 | async-start | bytes 9437184 | tf_op jit(solution)/shard_map/reduce_scatter | solution.py:238
  1158.9 8.0 copy-start.21
  1167.0 65.9 %copy-start.25 = (f32[1,2048]{1,0:T(1,128)S(1)}, f32[1,2048]{1,0:T(1,128)}, u32[]{:S(2)}) copy-start(f32[1,2048]{1,0:T(1,128)} %copy-done.24) | copy-start | bytes 24580
  1167.0 65.9 %copy-start.33 = (f32[256]{0:T(256)S(1)}, f32[256]{0:T(256)}, u32[]{:S(2)}) copy-start(f32[256]{0:T(256)} %copy-done.32) | copy-start | bytes 3076
  1167.0 65.9 %copy-start.41 = (f32[256]{0:T(256)S(1)}, f32[256]{0:T(256)}, u32[]{:S(2)}) copy-start(f32[256]{0:T(256)} %copy-done.40) | copy-start | bytes 3076
  1167.0 69.1 %copy-start.43 = (f32[256]{0:T(256)S(1)}, f32[256]{0:T(256)}, u32[]{:S(2)}) copy-start(f32[256]{0:T(256)} %copy-done.42) | copy-start | bytes 3076
  1167.0 69.2 %copy-start.39 = (f32[256]{0:T(256)S(1)}, f32[256]{0:T(256)}, u32[]{:S(2)}) copy-start(f32[256]{0:T(256)} %copy-done.38) | copy-start | bytes 3076
  (26 other events, 67.1 us)
Sparse Core Ops, SparseCore 0:
  15.0 57.0 all-gather.7
  74.0 54.3 all-gather.9
  130.3 65.6 all-gather.13
  198.3 54.3 all-gather.11
  316.7 71.2 reduce-scatter.5
  391.7 71.2 reduce-scatter.3
  471.4 54.3 all-gather.15
  527.4 383.0 all-gather.17
  913.7 245.2 all-reduce.6
  1162.7 70.1 reduce-scatter.7
